TPU v7x, 256 devices: a whole 4x4x8 slice. The times are simulated.
256 devices in a mesh: pair: 4 (over y_lo, core), col: 64 (over y_hi, x, z).
Axes of the slice: x: 4, y: 4 (y_hi: 2, y_lo: 2; y = y_hi * 2 + y_lo), z: 8, core: 2. Of those that a mesh axis runs over, the one named last changes fastest.
Arguments:
- amplitudes: bfloat16 [1536, 4096], P('pair', 'col'), may hold values from -6 to 6
- integrals: bfloat16 [4096, 81920], P('pair', 'col'), may hold values from -0.25 to 0.25
- irrep_start: int32 [9], replicated, may hold values from 0 to 4096, as said below
- pair_irrep: int32 [1536], P('pair'), may hold values from 0 to 7
Outputs:
- ladder: bfloat16 [1536, 81920], P('pair', 'col')
Inputs may be any that keep to these rules, and one draw needn't show every extreme that they name: Strictly rising multiples of 128; the first is 0 and the last is 4096; irrep j owns rows irrep_start[j] to irrep_start[j+1] - 1.
All inputs are finite; a program needn't handle non-finite values.
Results may differ from a plain program's by a relative error of at most 0.001.
Values may be sent and summed in bfloat16 or wider, within the bound.
A program may use at most 64 MiB of HBM per device.

v0:
```python
import jax
import jax.numpy as jnp
from jax import lax
from jax.sharding import PartitionSpec as P


def per_device(amplitudes, integrals, irrep_start, pair_irrep):
    local_rows = amplitudes.shape[1]
    first_row = lax.axis_index("col") * local_rows
    rows = first_row + jnp.arange(local_rows, dtype=jnp.int32)
    row_irrep = jnp.sum((rows[:, None] >= irrep_start[None, 1:8]).astype(jnp.int32), axis=1)
    keep = pair_irrep[:, None] == row_irrep[None, :]
    masked = jnp.where(keep, amplitudes, jnp.zeros_like(amplitudes))
    full_amp = lax.all_gather(masked, "col", axis=1, tiled=True)
    blocks = lax.all_to_all(full_amp, "pair", split_axis=1, concat_axis=0, tiled=True)
    summed = lax.psum_scatter(
        jnp.dot(blocks, integrals, preferred_element_type=jnp.float32),
        "pair",
        scatter_dimension=0,
        tiled=True,
    )
    return summed.astype(jnp.bfloat16)


def solution(mesh):
    placed = (P("pair", "col"), P("pair", "col"), P(), P("pair"))
    return jax.shard_map(
        per_device, mesh=mesh, in_specs=placed, out_specs=P("pair", "col"), check_vma=False
    )
```

profile of v0, /device:TPU:1, one launch (start us, length us, event | category | flops | bytes accessed | tf_op | source)
XLA Modules:
  0.0 277.6 jit_solution(218470783332346924)
XLA Ops:
  6.5 0.0 copy-start
  6.5 0.0 all-gather.2.cloned.1.call-start
  6.5 0.9 slice.3
  7.4 0.1 convert_reduce_fusion
  7.5 1.5 compare_select_fusion
  9.0 0.0 all-gather.2.cloned.1.call-update
  9.0 0.0 reduce-scatter.2.cloned.1.call-start
  9.1 125.1 %all-gather.2.cloned.1.call-done = bf16[384,4096]{0,1:T(8,128)(2,1)} async-done(((bf16[384,64]{0,1:T(8,128)(2,1)}), bf16[384,4096]{0,1:T(8,128)(2,1)}) %all-gather.2.cloned.1.call-update) | async-done | bytes 3145744 | tf_op jit(solution)/shard_map/all_gather | solution.py:14
  134.2 45.4 %all_to_all.19 = bf16[384,4,1024]{0,2,1:T(8,128)(2,1)} all-to-all(bf16[384,4,1024]{0,2,1:T(8,128)(2,1)} %bitcast.6), channel_id=1, replica_groups=mesh['pair'=4,'col'=64] {'pair'}, dimensions={1} | all-to-all | bytes 6291456 | tf_op jit(solution)/shard_map/all_to_all | solution.py:15
  179.5 4.7 %copy.6 = bf16[4,384,1024]{2,1,0:T(8,128)(2,1)} copy(bf16[4,384,1024]{1,2,0:T(8,128)(2,1)} %bitcast.5) | data formatting | bytes 6291456 | tf_op jit(solution)/shard_map/all_to_all | solution.py:15
  184.3 0.0 copy-done
  184.3 9.2 %fusion = f32[1536,1280]{1,0:T(8,128)} fusion(bf16[1536,1024]{1,0:T(8,128)(2,1)} %bitcast.7, bf16[1024,1280]{1,0:T(8,128)(2,1)S(1)} %copy-done), kind=kOutput, calls=%fused_computation.3 | convolution fusion | flops 4026531840 | bytes 13631488 | tf_op jit(solution)/shard_map/dot_general | solution.py:17
  193.5 0.0 reduce-scatter.2.cloned.1.call-update
  193.5 74.6 %reduce-scatter.2.cloned.1.call-done = f32[384,1280]{1,0:T(8,128)} async-done(((f32[1536,1280]{1,0:T(8,128)}), f32[384,1280]{1,0:T(8,128)}) %reduce-scatter.2.cloned.1.call-update) | async-done | bytes 1966096 | tf_op jit(solution)/shard_map/reduce_scatter | solution.py:16
  268.1 2.6 convert_element_type.7
  (1 shorter events, 0.0 us)
Async XLA Ops:
  6.5 177.7 %copy-start = (bf16[1024,1280]{1,0:T(8,128)(2,1)S(1)}, bf16[1024,1280]{1,0:T(8,128)(2,1)}, u32[]{:S(2)}) copy-start(bf16[1024,1280]{1,0:T(8,128)(2,1)} %param.5) | copy-start | bytes 7864324
  6.5 127.6 %all-gather.2.cloned.1.call-start = ((), (), s32[]{:S(2)}) async-start(), calls=%async_computation.2 | async-start | bytes 3194880 | tf_op jit(solution)/shard_map/all_gather | solution.py:14
  9.0 259.1 %reduce-scatter.2.cloned.1.call-start = ((), (), s32[]{:S(2)}) async-start(), calls=%async_computation.3 | async-start | bytes 9830400 | tf_op jit(solution)/shard_map/reduce_scatter | solution.py:16
Sparse Core Ops, SparseCore 0:
  11.0 123.0 all-gather.1
  193.6 74.4 reduce-scatter.1
where the time goes:
time: 278 us
  waiting for transfers between devices  200 us (72%)
  blocking collectives  45.4 us (16%)
  between operations  13.4 us (5%)
  matrix products  9.23 us (3%)
  local copies, waits for them, and re-layouts  5.62 us (2%)
  other arithmetic  4.18 us (2%)
    all_gather x1, waiting for transfers between devices, per_device(): full_amp = lax.all_gather(masked, 'col', axis=1, tiled=True)  125 us
    reduce_scatter x1, waiting for transfers between devices, per_device(): lax.psum_scatter(jnp.dot(blocks, integrals, preferred_element_type=jnp.fl...  74.6 us
    all_to_all x1, blocking collectives, per_device(): lax.all_to_all(full_amp, 'pair', split_axis=1, concat_axis=0, tiled=True)  45.4 us
    dot_general x1, matrix products, per_device(): jnp.dot(blocks, integrals, preferred_element_type=jnp.float32)  9.23 us
  transfers between devices with their start and end apart: 2, of which 2 were waited for; matrix products, arithmetic and copies ran while one was open for 0% of the time, Pallas kernels for 0%

commit v1 on v0

--- a/solution.py
+++ b/solution.py
@@ -11,7 +11,15 @@
     row_irrep = jnp.sum((rows[:, None] >= irrep_start[None, 1:8]).astype(jnp.int32), axis=1)
     keep = pair_irrep[:, None] == row_irrep[None, :]
     masked = jnp.where(keep, amplitudes, jnp.zeros_like(amplitudes))
-    full_amp = lax.all_gather(masked, "col", axis=1, tiled=True)
+    full_amp = jnp.concatenate(
+        lax.all_to_all(
+            jnp.stack([masked for _ in range(lax.psum(1, axis_name="col"))], axis=0),
+            axis_name="col",
+            split_axis=0,
+            concat_axis=0,
+        ),
+        axis=1,
+    )
     blocks = lax.all_to_all(full_amp, "pair", split_axis=1, concat_axis=0, tiled=True)
     summed = lax.psum_scatter(
         jnp.dot(blocks, integrals, preferred_element_type=jnp.float32),

time: 278 us -> 236 us (0.85)
  waiting for transfers between devices: 200 us -> 74 us
  blocking collectives: 45.4 us -> 130 us
    all_gather x1 -> x0, waiting for transfers between devices: 125 us -> none  [per_device(): full_amp = lax.all_gather(masked, 'col', axis=1, tiled=True)]
    all_to_all x0 -> x1, blocking collectives: none -> 87.9 us  [per_device(): lax.all_to_all(jnp.stack([masked for _ in range(lax.psum(1, axis_name='co...]
    all_to_all x1, blocking collectives: 45.4 us -> 41.7 us  [per_device(): lax.all_to_all(full_amp, 'pair', split_axis=1, concat_axis=0, tiled=True)]
  transfers between devices with their start and end apart: 2 -> 1, of which waited for: 2 -> 1; matrix products, arithmetic and copies ran while one was open for 0% -> 0% of each run, Pallas kernels for 0% -> 0%
where the time goes in v1:
time: 236 us
  blocking collectives  130 us (55%)
  waiting for transfers between devices  74 us (31%)
  between operations  13.4 us (6%)
  matrix products  9.23 us (4%)
  local copies, waits for them, and re-layouts  6.1 us (3%)
  other arithmetic  3.56 us (2%)
    all_to_all x1, blocking collectives, per_device(): lax.all_to_all(jnp.stack([masked for _ in range(lax.psum(1, axis_name='co...  87.9 us
    reduce_scatter x1, waiting for transfers between devices, per_device(): lax.psum_scatter(jnp.dot(blocks, integrals, preferred_element_type=jnp.fl...  74 us
    all_to_all x1, blocking collectives, per_device(): lax.all_to_all(full_amp, 'pair', split_axis=1, concat_axis=0, tiled=True)  41.7 us
    dot_general x1, matrix products, per_device(): jnp.dot(blocks, integrals, preferred_element_type=jnp.float32)  9.23 us
    all_to_all x1, local copies, waits for them, and re-layouts, per_device(): lax.all_to_all(full_amp, 'pair', split_axis=1, concat_axis=0, tiled=True)  4.73 us
  transfers between devices with their start and end apart: 1, of which 1 were waited for; matrix products, arithmetic and copies ran while one was open for 0% of the time, Pallas kernels for 0%

profile of v1, /device:TPU:1, one launch (start us, length us, event | category | flops | bytes accessed | tf_op | source)
XLA Modules:
  0.0 235.9 jit_solution(12534893899338710685)
XLA Ops:
  6.5 0.0 copy-start
  6.5 0.0 reduce-scatter.2.cloned.1.call-start
  6.5 0.9 slice.3
  7.4 0.1 convert_reduce_fusion
  7.5 0.9 compare_select_fusion
  8.4 0.5 stack.2
  8.9 87.9 %all_to_all.24 = bf16[64,384,64]{1,2,0:T(8,128)(2,1)S(1)} all-to-all(bf16[64,384,64]{1,2,0:T(8,128)(2,1)S(1)} %stack.2), channel_id=1, replica_groups=mesh['pair'=4,'col'=64] {'col'}, dimensions={0} | all-to-all | bytes 6291456 | tf_op jit(solution)/shard_map/all_to_all | solution.py:15
  96.8 41.7 %all_to_all.25 = bf16[384,4,1024]{0,2,1:T(8,128)(2,1)} all-to-all(bf16[384,4,1024]{0,2,1:T(8,128)(2,1)S(1)} %bitcast.7), channel_id=1, replica_groups=mesh['pair'=4,'col'=64] {'pair'}, dimensions={1} | all-to-all | bytes 6291456 | tf_op jit(solution)/shard_map/all_to_all | solution.py:23
  138.5 4.7 %copy.7 = bf16[4,384,1024]{2,1,0:T(8,128)(2,1)} copy(bf16[4,384,1024]{1,2,0:T(8,128)(2,1)} %bitcast.8) | data formatting | bytes 6291456 | tf_op jit(solution)/shard_map/all_to_all | solution.py:23
  143.2 0.0 copy-done
  143.2 9.2 %fusion = f32[1536,1280]{1,0:T(8,128)} fusion(bf16[1536,1024]{1,0:T(8,128)(2,1)} %bitcast.9, bf16[1024,1280]{1,0:T(8,128)(2,1)S(1)} %copy-done), kind=kOutput, calls=%fused_computation.3 | convolution fusion | flops 4026531840 | bytes 13631488 | tf_op jit(solution)/shard_map/dot_general | solution.py:25
  152.4 0.0 reduce-scatter.2.cloned.1.call-update
  152.5 74.0 %reduce-scatter.2.cloned.1.call-done = f32[384,1280]{1,0:T(8,128)} async-done(((f32[1536,1280]{1,0:T(8,128)}), f32[384,1280]{1,0:T(8,128)}) %reduce-scatter.2.cloned.1.call-update) | async-done | bytes 1966096 | tf_op jit(solution)/shard_map/reduce_scatter | solution.py:24
  226.4 2.6 %convert_element_type.7 = bf16[384,1280]{1,0:T(8,128)(2,1)} convert(f32[384,1280]{1,0:T(8,128)} %reduce-scatter.2.cloned.1.call-done) | non-fusion elementwise | flops 491520 | bytes 2949120 | tf_op jit(solution)/shard_map/convert_element_type | solution.py:30
  (1 shorter events, 0.0 us)
Async XLA Ops:
  6.5 136.7 %copy-start = (bf16[1024,1280]{1,0:T(8,128)(2,1)S(1)}, bf16[1024,1280]{1,0:T(8,128)(2,1)}, u32[]{:S(2)}) copy-start(bf16[1024,1280]{1,0:T(8,128)(2,1)} %param.5) | copy-start | bytes 7864324
  6.5 219.9 %reduce-scatter.2.cloned.1.call-start = ((), (), s32[]{:S(2)}) async-start(), calls=%async_computation.3 | async-start | bytes 9830400 | tf_op jit(solution)/shard_map/reduce_scatter | solution.py:24
Sparse Core Ops, SparseCore 0:
  152.6 73.8 reduce-scatter.1
